TPU v7x, 256 devices: a whole 4x4x8 slice. The times are simulated.
256 devices in a mesh: dp: 4 (over y), tensor: 64 (over x, z, core).
Axes of the slice: x: 4, y: 4, z: 8, core: 2. Of those that a mesh axis runs over, the one named last changes fastest.
Arguments:
- tokens: bfloat16 [4, 8192, 1536], P('dp', 'tensor'), may hold values from -6 to 6
- attn_gain: float32 [1536], replicated, may hold values from 0.1 to 1.9
- qkv_weight: bfloat16 [1536, 2560], P(None, 'dp'), may hold values from -0.25 to 0.25
- out_weight: bfloat16 [1536, 1536], P('dp'), may hold values from -0.15625 to 0.15625
- prefix_cache: bfloat16 [4, 512, 2, 512], P('dp', 'tensor'), may hold values from -640 to 640
- lengths: int32 [4, 256], P('dp'), may hold values from 1 to 384, 8192 in all within a row
- ffn_gain: float32 [1536], replicated, may hold values from 0.1 to 1.9
- expert_ids: int32 [4, 8192, 8], P('dp', 'tensor'), may hold values from 0 to 31, all different within a row; in each aligned block of 128 rows (0 to 127, 128 to 255, ..., all dimensions but the last counted through in order) at most 40 rows name the same one
- gate_weights: float32 [4, 8192, 8], P('dp', 'tensor'), may hold values from 0.05 to 0.5
- expert_in: bfloat16 [64, 1536, 512], P('tensor'), may hold values from -0.15625 to 0.15625
- expert_out: bfloat16 [64, 256, 1536], P('tensor'), may hold values from -0.25 to 0.25
Outputs:
- hidden_state: bfloat16 [4, 8192, 1536], P('dp', 'tensor')
- mixed: bfloat16 [4, 8192, 1536], P('dp', 'tensor')
Inputs may be any that keep to these rules, and one draw needn't show every extreme that they name: `lengths`: each group's 256 requests fill its 8192 suffix positions in order, and the longest holds exactly 384 tokens. `expert_ids`: each token names 8 different experts; among the 128 tokens of one device no expert is named more than 40 times, a bound that some block reaches.
All inputs are finite; a program needn't handle non-finite values.
Results may differ from a plain program's by a relative error of at most 0.014.
The roundings to bfloat16 on the way count: a program that leaves them out, or rounds other values in their place, can miss the bound.
Values may be sent and summed in bfloat16 or wider, within the bound.
No kernel may reach another device: no remote copies, remote signals or barrier semaphores. Data moves between devices by JAX's collectives and lax.ppermute only.
A program may use at most 128 MiB of HBM per device.

v0:
```python
import jax
import jax.numpy as jnp
from jax import lax
from jax.sharding import PartitionSpec as P

HEADS = 24
KV_HEADS = 8
HEAD_DIM = 64
EXPERTS = 32
TOPK = 8
SHIFTS = 2
CAP = 40
TENSOR = ("chip", "core")
EPS = 1e-06
THETA = 10000.0


def from_behind(value, axis, steps):
    count = lax.axis_size(axis)
    first, last = (max(0, -steps), min(count, count - steps))
    return lax.ppermute(value, axis, [(source, source + steps) for source in range(first, last)])


def rms_norm(x, gain):
    values = x.astype(jnp.float32)
    mean_sq = jnp.mean(values * values, axis=-1, keepdims=True)
    return (values * lax.rsqrt(mean_sq + EPS) * gain).astype(jnp.bfloat16)


def rotary(x, positions):
    half = x.shape[-1] // 2
    freqs = THETA ** (-jnp.arange(half, dtype=jnp.float32) * 2.0 / x.shape[-1])
    angles = positions.astype(jnp.float32)[:, None] * freqs[None, :]
    cosine = jnp.concatenate([jnp.cos(angles), jnp.cos(angles)], axis=-1)[:, None, :]
    sine = jnp.concatenate([jnp.sin(angles), jnp.sin(angles)], axis=-1)[:, None, :]
    turned = jnp.concatenate([-x[..., half:], x[..., :half]], axis=-1)
    return x * cosine + turned * sine


def request_info(index, lengths):
    ends = jnp.cumsum(lengths, dtype=jnp.int32)
    before = ends[None, :] <= index[:, None]
    segment = jnp.sum(before.astype(jnp.int32), axis=1, dtype=jnp.int32)
    start = jnp.sum(jnp.where(before, lengths[None, :], 0), axis=1, dtype=jnp.int32)
    return (segment, index - start)


def merge_block(carry, scores, values, visible):
    best, total, acc = carry
    if visible is not None:
        scores = jnp.where(visible, scores, -1e30)
    newest = jnp.maximum(best, jnp.max(scores, axis=-1))
    probs = jnp.exp(scores - newest[..., None])
    if visible is not None:
        probs = jnp.where(visible, probs, 0.0)
    decay = jnp.exp(best - newest)
    total = total * decay + jnp.sum(probs, axis=-1)
    acc = acc * decay[..., None] + jnp.einsum(
        "tgrn,ngd->tgrd", probs.astype(jnp.bfloat16), values, preferred_element_type=jnp.float32
    )
    return (newest, total, acc)


def shards(
    tokens,
    attn_gain,
    qkv_weight,
    out_weight,
    prefix_cache,
    lengths,
    ffn_gain,
    expert_ids,
    gate_weights,
    expert_in,
    expert_out,
):
    rows = tokens.shape[1]
    model = tokens.shape[2]
    head_cols = HEADS * HEAD_DIM
    kv_cols = KV_HEADS * HEAD_DIM
    ratio = HEADS // KV_HEADS
    scale = 1.0 / HEAD_DIM**0.5
    lanes = lax.axis_size(TENSOR)
    prefix_len = prefix_cache.shape[1] * lanes
    own_lengths = lengths[0]
    inputs = tokens[0]
    normed = rms_norm(inputs, attn_gain)
    full_qkv, full_out = (
        lax.all_gather(qkv_weight, "dp", axis=1, tiled=True),
        lax.all_gather(out_weight, "dp", axis=0, tiled=True),
    )
    qkv = jnp.dot(normed, full_qkv, preferred_element_type=jnp.float32).astype(jnp.bfloat16)
    lane = lax.axis_index(TENSOR)
    q_index = lane * rows + jnp.arange(rows, dtype=jnp.int32)
    q_segment, offset = request_info(q_index, own_lengths)
    positions = prefix_len + offset
    query = rotary(
        qkv[:, :head_cols].astype(jnp.float32).reshape(rows, HEADS, HEAD_DIM), positions
    ).astype(jnp.bfloat16)
    query = query.reshape(rows, KV_HEADS, ratio, HEAD_DIM)
    keys = rotary(
        qkv[:, head_cols : head_cols + kv_cols]
        .astype(jnp.float32)
        .reshape(rows, KV_HEADS, HEAD_DIM),
        positions,
    ).astype(jnp.bfloat16)
    local_pairs = jnp.stack([keys.reshape(rows, kv_cols), qkv[:, head_cols + kv_cols :]], axis=1)
    start_carry = (
        jnp.full((rows, KV_HEADS, ratio), -1e30, jnp.float32),
        jnp.zeros((rows, KV_HEADS, ratio), jnp.float32),
        jnp.zeros((rows, KV_HEADS, ratio, HEAD_DIM), jnp.float32),
    )
    piece = lax.all_gather(prefix_cache[0], TENSOR, axis=0, tiled=True)
    count = piece.shape[0]
    cached_keys = piece[:, 0].reshape(count, KV_HEADS, HEAD_DIM)
    cached_values = piece[:, 1].reshape(count, KV_HEADS, HEAD_DIM)
    scores = (
        jnp.einsum("tgrd,ngd->tgrn", query, cached_keys, preferred_element_type=jnp.float32) * scale
    )
    carry = merge_block(start_carry, scores, cached_values, None)
    window = local_pairs[None]
    for bit in range(SHIFTS):
        earlier = from_behind(window, TENSOR, 2**bit)
        window = jnp.concatenate([window, earlier], axis=0)
    depth = window.shape[0]
    k_index = (
        (lane - jnp.arange(depth, dtype=jnp.int32))[:, None] * rows
        + jnp.arange(rows, dtype=jnp.int32)[None, :]
    ).reshape(-1)
    k_segment, unused = request_info(k_index, own_lengths)
    visible = (
        (k_index[None, :] >= 0)
        & (k_index[None, :] <= q_index[:, None])
        & (k_segment[None, :] == q_segment[:, None])
    )
    suffix_pairs = window.reshape(depth * rows, 2, kv_cols)
    suffix_keys = suffix_pairs[:, 0].reshape(depth * rows, KV_HEADS, HEAD_DIM)
    suffix_values = suffix_pairs[:, 1].reshape(depth * rows, KV_HEADS, HEAD_DIM)
    scores = (
        jnp.einsum("tgrd,ngd->tgrn", query, suffix_keys, preferred_element_type=jnp.float32) * scale
    )
    best, total, acc = merge_block(carry, scores, suffix_values, visible[:, None, None, :])
    attended = (acc / total[..., None]).astype(jnp.bfloat16).reshape(rows, head_cols)
    projected = jnp.dot(attended, full_out, preferred_element_type=jnp.float32)
    hidden_state = (inputs.astype(jnp.float32) + projected).astype(jnp.bfloat16)
    moe_input = rms_norm(hidden_state, ffn_gain)
    chips = lax.axis_size("chip")
    unit_ff = expert_in.shape[2] // 2
    flat_ids = expert_ids[0].reshape(-1)
    onehot = (flat_ids[:, None] == jnp.arange(EXPERTS, dtype=jnp.int32)[None, :]).astype(jnp.int32)
    earlier_count = jnp.cumsum(onehot, axis=0, dtype=jnp.int32) - onehot
    slots = jnp.sum(earlier_count * onehot, axis=1, dtype=jnp.int32)
    target = flat_ids * CAP + slots
    row_of = jnp.repeat(jnp.arange(rows, dtype=jnp.int32), TOPK)
    source = jnp.full((chips * CAP,), rows, jnp.int32).at[target].set(row_of)
    padded_input = jnp.concatenate([moe_input, jnp.zeros((1, model), jnp.bfloat16)], axis=0)
    outgoing = padded_input[source].reshape(chips, CAP, model)
    arrived = lax.all_to_all(outgoing, "chip", 0, 0, tiled=True)
    sibling = lax.ppermute(arrived, "core", [(0, 1), (1, 0)])
    unit_rows = jnp.concatenate([arrived, sibling], axis=0).reshape(2 * chips * CAP, model)
    inner = jnp.dot(unit_rows, expert_in[0], preferred_element_type=jnp.float32)
    activated = (jax.nn.silu(inner[:, :unit_ff]) * inner[:, unit_ff:]).astype(jnp.bfloat16)
    produced = jnp.dot(activated, expert_out[0], preferred_element_type=jnp.float32).astype(
        jnp.bfloat16
    )
    produced = produced.reshape(2, chips, CAP, model)
    partner = lax.ppermute(produced[1], "core", [(0, 1), (1, 0)])
    summed = (produced[0].astype(jnp.float32) + partner.astype(jnp.float32)).astype(jnp.bfloat16)
    returned = lax.all_to_all(summed, "chip", 0, 0, tiled=True)
    picked = returned.reshape(chips * CAP, model)[target].reshape(rows, TOPK, model)
    combined = jnp.einsum("tk,tkd->td", gate_weights[0], picked.astype(jnp.float32))
    mixed = (hidden_state.astype(jnp.float32) + combined).astype(jnp.bfloat16)
    return (hidden_state[None], mixed[None])


def solution(mesh):
    groups, lanes = mesh.devices.shape
    chip_mesh = jax.sharding.Mesh(
        mesh.devices.reshape(groups, lanes // 2, 2), ("dp", "chip", "core")
    )
    in_specs = (
        P("dp", TENSOR, None),
        P(),
        P(None, "dp"),
        P("dp", None),
        P("dp", TENSOR, None, None),
        P("dp", None),
        P(),
        P("dp", TENSOR, None),
        P("dp", TENSOR, None),
        P(TENSOR, None, None),
        P(TENSOR, None, None),
    )
    out_specs = (P("dp", TENSOR, None), P("dp", TENSOR, None))
    return jax.shard_map(
        shards, mesh=chip_mesh, in_specs=in_specs, out_specs=out_specs, check_vma=False
    )
```

profile of v0, /device:TPU:34, one launch (start us, length us, event | category | flops | bytes accessed | tf_op | source)
XLA Modules:
  0.0 489.5 jit_solution(2247679255793934085)
XLA Ops:
  9.6 0.8 copy.67
  11.3 1.0 reduce-window.15
  12.6 0.8 fusion.59
  13.4 1.2 fusion.47
  14.9 9.0 %reduce-window.19 = s32[32,8,128]{2,1,0:T(8,128)S(1)} reduce-window(s32[32,8,128]{2,1,0:T(8,128)S(1)} %fusion.64, s32[]{:T(128)} %constant.27.clone.1), window={size=1x1x128 pad=0_0x0_0x127_0}, to_apply=%region_11.12 | reduce-window | flops 4161536 | bytes 262148 | tf_op jit(solution)/shard_map/reduce-window.2
  24.7 4.3 scatter_custom_fusion
  29.2 0.9 compare_and_fusion
  30.9 57.8 %all-gather.9.cloned.1.call-done = bf16[1,512,2,512]{3,2,0,1:T(2,128)(2,1)} async-done(((bf16[1,8,2,512]{3,2,0,1:T(2,128)(2,1)}), bf16[1,512,2,512]{3,2,0,1:T(2,128)(2,1)}) %all-gather.9.cloned.1.call-update) | async-done | bytes 1048592 | tf_op jit(solution)/shard_map/all_gather | solution.py:113
  88.7 4.3 fusion.74
  92.9 3.5 copy.57
  96.4 3.5 copy.58
  99.9 71.2 %all-gather.5.cloned.1.call-done = bf16[1536,2560]{1,0:T(8,128)(2,1)} async-done(((bf16[1536,640]{1,0:T(8,128)(2,1)}), bf16[1536,2560]{1,0:T(8,128)(2,1)}) %all-gather.5.cloned.1.call-update) | async-done | bytes 7864336 | tf_op jit(solution)/shard_map/all_gather | solution.py:89
  171.1 4.5 convolution_convert_fusion.1
  175.8 0.8 maximum_multiply_fusion.1
  176.8 0.7 maximum_bitcast_fusion
  177.5 1.9 collective-permute-start
  179.9 5.7 %collective-permute-done = bf16[1,128,2,512]{3,1,2,0:T(8,128)(2,1)} collective-permute-done((bf16[1,128,2,512]{3,1,2,0:T(8,128)(2,1)}, bf16[1,128,2,512]{3,1,2,0:T(8,128)(2,1)}, u32[]{:S(2)}, u32[]{:S(2)}) %collective-permute-start) | collective-permute-done | bytes 262176 | tf_op jit(solution)/shard_map/ppermute | solution.py:21
  185.5 1.1 pad_maximum_fusion.2
  186.7 3.6 collective-permute-start.1
  190.3 0.9 fusion.51
  191.3 4.8 bitcast_reduce_fusion
  196.0 5.5 %collective-permute-done.1 = bf16[2,128,2,512]{3,1,2,0:T(8,128)(2,1)S(1)} collective-permute-done((bf16[2,128,2,512]{3,1,2,0:T(8,128)(2,1)S(1)}, bf16[2,128,2,512]{3,1,2,0:T(8,128)(2,1)S(1)}, u32[]{:S(2)}, u32[]{:S(2)}) %collective-permute-start.1) | collective-permute-done | bytes 524320 | tf_op jit(solution)/shard_map/ppermute | solution.py:21
  201.6 1.1 pad_maximum_fusion.1
  202.8 1.1 fusion.75
  203.9 1.3 copy.63
  205.1 2.1 copy.64
  207.2 1.1 fusion.2
  208.3 3.7 fusion.3
  212.0 1.5 fusion.5
  213.6 1.7 fusion.22
  215.3 0.7 slice-done
  216.6 1.7 fusion.40
  218.3 10.7 %all-gather.7.cloned.1.call-done = bf16[1536,1536]{1,0:T(8,128)(2,1)} async-done(((bf16[384,1536]{1,0:T(8,128)(2,1)}), bf16[1536,1536]{1,0:T(8,128)(2,1)}) %all-gather.7.cloned.1.call-update) | async-done | bytes 4718608 | tf_op jit(solution)/shard_map/all_gather | solution.py:90
  229.0 3.2 fusion.43
  232.5 5.4 %gather_fusion = bf16[1280,1536]{1,0:T(8,128)(2,1)} fusion(bf16[129,1536]{1,0:T(8,128)(2,1)S(1)} %concatenate.40, s32[2048]{0:T(1024)S(1)} %pad_clamp_fusion), kind=kCustom, calls=%fused_computation | custom fusion | bytes 7869440 | tf_op jit(solution)/shard_map/gather | solution.py:157
  237.9 99.6 %all_to_all.10 = bf16[32,40,1536]{2,1,0:T(8,128)(2,1)S(1)} all-to-all(bf16[32,40,1536]{2,1,0:T(8,128)(2,1)} %bitcast.159), channel_id=1, replica_groups=mesh['dp'=4,'chip'=32,'core'=2] {'chip'}, dimensions={0} | all-to-all | bytes 7864320 | tf_op jit(solution)/shard_map/all_to_all | solution.py:158
  337.5 2.0 copy-done.2
  339.5 6.9 %collective-permute-done.2 = bf16[32,40,1536]{2,1,0:T(8,128)(2,1)} collective-permute-done((bf16[32,40,1536]{2,1,0:T(8,128)(2,1)S(1)}, bf16[32,40,1536]{2,1,0:T(8,128)(2,1)}, u32[]{:S(2)}, u32[]{:S(2)}) %collective-permute-start.2) | collective-permute-done | bytes 3932192 | tf_op jit(solution)/shard_map/ppermute | solution.py:159
  346.4 7.1 %pad_maximum_fusion = bf16[64,40,1536]{2,1,0:T(8,128)(2,1)} fusion(bf16[32,40,1536]{2,1,0:T(8,128)(2,1)} %collective-permute-done.2, bf16[32,40,1536]{2,1,0:T(8,128)(2,1)} %copy-done.2), kind=kLoop, calls=%fused_computation.4 | loop fusion | flops 3932160 | bytes 15728640 | tf_op jit(solution)/shard_map/concatenate | solution.py:160
  353.4 6.6 %fusion.18 = f32[2560,512]{1,0:T(8,128)S(1)} fusion(bf16[2560,1536]{1,0:T(8,128)(2,1)} %bitcast.161, bf16[1,1536,512]{2,1,0:T(8,128)(2,1)S(1)} %copy-done), kind=kOutput, calls=%fused_computation.29 | convolution fusion | flops 4026531840 | bytes 14680064 | tf_op jit(solution)/shard_map/dot_general | solution.py:161
  360.1 2.3 convolution_convert_fusion
  363.1 6.7 %collective-permute-done.3 = bf16[32,40,1536]{2,1,0:T(8,128)(2,1)S(1)} collective-permute-done((bf16[32,40,1536]{2,1,0:T(8,128)(2,1)S(1)}, bf16[32,40,1536]{2,1,0:T(8,128)(2,1)S(1)}, u32[]{:S(2)}, u32[]{:S(2)}) %collective-permute-start.3) | collective-permute-done | bytes 3932192 | tf_op jit(solution)/shard_map/ppermute | solution.py:167
  369.8 3.0 fusion
  372.8 6.0 %all-to-all-start.1 = ((bf16[32,40,1536]{2,1,0:T(8,128)(2,1)}), bf16[32,40,1536]{2,1,0:T(8,128)(2,1)}, u32[]{:S(2)}, u32[]{:S(2)}) async-start(bf16[32,40,1536]{2,1,0:T(8,128)(2,1)} %fusion), calls=%async_computation.1 | async-start | bytes 7864320 | tf_op jit(solution)/shard_map/all_to_all | solution.py:169
  378.9 90.3 %all-to-all-done.1 = bf16[32,40,1536]{2,1,0:T(8,128)(2,1)} async-done(((bf16[32,40,1536]{2,1,0:T(8,128)(2,1)}), bf16[32,40,1536]{2,1,0:T(8,128)(2,1)}, u32[]{:S(2)}, u32[]{:S(2)}) %all-to-all-start.1) | async-done | bytes 3932192 | tf_op jit(solution)/shard_map/all_to_all | solution.py:169
  469.2 10.0 %gather_fusion.1 = bf16[1024,1536]{1,0:T(8,128)(2,1)} fusion(bf16[1280,1536]{1,0:T(8,128)(2,1)} %bitcast.47, s32[1024]{0:T(1024)S(1)} %broadcast_clamp_fusion), kind=kCustom, calls=%fused_computation.1 | custom fusion | bytes 6295552 | tf_op jit(solution)/shard_map/gather | solution.py:170
  479.2 2.8 fusion.9
  482.1 0.8 fusion.54
  (88 shorter events, 8.2 us)
Async XLA Ops:
  7.2 346.3 %copy-start = (bf16[1,1536,512]{2,1,0:T(8,128)(2,1)S(1)}, bf16[1,1536,512]{2,1,0:T(8,128)(2,1)}, u32[]{:S(2)}) copy-start(bf16[1,1536,512]{2,1,0:T(8,128)(2,1)} %param.20) | copy-start | bytes 4718596
  7.2 81.5 %all-gather.9.cloned.1.call-start = ((), (), s32[]{:S(2)}) async-start(), calls=%async_computation.4 | async-start | bytes 1064960 | tf_op jit(solution)/shard_map/all_gather | solution.py:113
  7.9 163.2 %all-gather.5.cloned.1.call-start = ((), (), s32[]{:S(2)}) async-start(), calls=%async_computation.2 | async-start | bytes 9830400 | tf_op jit(solution)/shard_map/all_gather | solution.py:89
  8.7 162.5 %copy-start.3 = (bf16[1,128,1536]{2,1,0:T(8,128)(2,1)S(1)}, bf16[1,128,1536]{2,1,0:T(8,128)(2,1)}, u32[]{:S(2)}) copy-start(bf16[1,128,1536]{2,1,0:T(8,128)(2,1)} %param.11) | copy-start | bytes 1179652
  8.7 162.4 %copy-start.9 = (f32[1536]{0:T(1024)S(1)}, f32[1536]{0:T(1024)}, u32[]{:S(2)}) copy-start(f32[1536]{0:T(1024)} %param.12) | copy-start | bytes 18436
  8.7 220.3 %all-gather.7.cloned.1.call-start = ((), (), s32[]{:S(2)}) async-start(), calls=%async_computation.3 | async-start | bytes 5898240 | tf_op jit(solution)/shard_map/all_gather | solution.py:90
  30.7 69.2 %copy-start.8 = (f32[128,64]{0,1:T(8,128)}, f32[128,64]{0,1:T(8,128)S(1)}, u32[]{:S(2)}) copy-start(f32[128,64]{0,1:T(8,128)S(1)} %get-tuple-element.29) | copy-start | bytes 98308
  177.5 8.0 %collective-permute-start = (bf16[1,128,2,512]{3,1,2,0:T(8,128)(2,1)}, bf16[1,128,2,512]{3,1,2,0:T(8,128)(2,1)}, u32[]{:S(2)}, u32[]{:S(2)}) collective-permute-start(bf16[1,128,2,512]{3,1,2,0:T(8,128)(2,1)} %maximum_bitcast_fusion), channel_id=1, source_target_pairs={{0,1},{1,2},{2,3},{3,4},{4,5},{5,6},{6,7},{7,8},{8,9},{9,10},{10,1... | collective-permute-start | bytes 786440 | tf_op jit(solution)/shard_map/ppermute | solution.py:21
  186.7 14.9 %collective-permute-start.1 = (bf16[2,128,2,512]{3,1,2,0:T(8,128)(2,1)S(1)}, bf16[2,128,2,512]{3,1,2,0:T(8,128)(2,1)S(1)}, u32[]{:S(2)}, u32[]{:S(2)}) collective-permute-start(bf16[2,128,2,512]{3,1,2,0:T(8,128)(2,1)S(1)} %pad_maximum_fusion.2), channel_id=1, source_target_pairs={{0,2},{1,3},{2,4},{3,5},{4,6},{5,7},{6,8},{7,9},{8,10},{9,11},{10,... | collective-permute-start | bytes 1572872 | tf_op jit(solution)/shard_map/ppermute | solution.py:21
  191.2 16.0 %copy-start.5 = (pred[128,512]{0,1:T(8,128)(4,1)S(1)}, pred[128,512]{0,1:T(8,128)(4,1)}, u32[]{:S(2)}) copy-start(pred[128,512]{0,1:T(8,128)(4,1)} %compare_and_fusion) | copy-start | bytes 196612
  208.3 5.2 %copy-start.7 = (bf16[512,1,512]{0,2,1:T(8,128)(2,1)S(1)}, bf16[512,1,512]{0,2,1:T(8,128)(2,1)}, u32[]{:S(2)}) copy-start(bf16[512,1,512]{0,2,1:T(8,128)(2,1)} %copy.64) | copy-start | bytes 1572868
  213.5 2.4 slice-start
  213.5 2.4 copy-start.6
  213.6 3.1 slice-start.1
  216.6 15.6 %copy-start.10 = (f32[1536]{0:T(1024)S(1)}, f32[1536]{0:T(1024)}, u32[]{:S(2)}) copy-start(f32[1536]{0:T(1024)} %param.17) | copy-start | bytes 18436
  232.2 249.9 %copy-start.4 = (bf16[128,1536]{1,0:T(8,128)(2,1)}, bf16[128,1536]{1,0:T(8,128)(2,1)S(1)}, u32[]{:S(2)}) copy-start(bf16[128,1536]{1,0:T(8,128)(2,1)S(1)} %get-tuple-element.28) | copy-start | bytes 1179652
  337.5 2.0 copy-start.2
  339.5 6.9 %collective-permute-start.2 = (bf16[32,40,1536]{2,1,0:T(8,128)(2,1)S(1)}, bf16[32,40,1536]{2,1,0:T(8,128)(2,1)}, u32[]{:S(2)}, u32[]{:S(2)}) collective-permute-start(bf16[32,40,1536]{2,1,0:T(8,128)(2,1)S(1)} %all_to_all.10), channel_id=1, source_target_pairs={{0,1},{1,0},{2,3},{3,2},{4,5},{5,4},{6,7},{7,6},{8,9},{9,8},{10,11... | collective-permute-start | bytes 11796488 | tf_op jit(solution)/shard_map/ppermute | solution.py:159
  353.4 6.6 %copy-start.12 = (bf16[1,256,1536]{2,1,0:T(8,128)(2,1)S(1)}, bf16[1,256,1536]{2,1,0:T(8,128)(2,1)}, u32[]{:S(2)}) copy-start(bf16[1,256,1536]{2,1,0:T(8,128)(2,1)} %param.21) | copy-start | bytes 2359300
  362.9 6.9 %collective-permute-start.3 = (bf16[32,40,1536]{2,1,0:T(8,128)(2,1)S(1)}, bf16[32,40,1536]{2,1,0:T(8,128)(2,1)S(1)}, u32[]{:S(2)}, u32[]{:S(2)}) collective-permute-start(bf16[32,40,1536]{2,1,0:T(8,128)(2,1)S(1)} %bitcast.166), channel_id=1, source_target_pairs={{0,1},{1,0},{2,3},{3,2},{4,5},{5,4},{6,7},{7,6},{8,9},{9,8},{10,11... | collective-permute-start | bytes 11796488 | tf_op jit(solution)/shard_map/ppermute | solution.py:167
  372.8 6.0 %copy-start.11 = (f32[1,128,8]{1,2,0:T(8,128)S(1)}, f32[1,128,8]{1,2,0:T(8,128)}, u32[]{:S(2)}) copy-start(f32[1,128,8]{1,2,0:T(8,128)} %param.19) | copy-start | bytes 12292
  372.8 96.5 %all-to-all-start.1 = ((bf16[32,40,1536]{2,1,0:T(8,128)(2,1)}), bf16[32,40,1536]{2,1,0:T(8,128)(2,1)}, u32[]{:S(2)}, u32[]{:S(2)}) async-start(bf16[32,40,1536]{2,1,0:T(8,128)(2,1)} %fusion), calls=%async_computation.1 | async-start | bytes 7864320 | tf_op jit(solution)/shard_map/all_to_all | solution.py:169
  469.2 13.7 %copy-start.1 = (bf16[1,1536,512]{2,1,0:T(8,128)(2,1)S(1)}, bf16[1,1536,512]{2,1,0:T(8,128)(2,1)}, u32[]{:S(2)}) copy-start(bf16[1,1536,512]{2,1,0:T(8,128)(2,1)} %param.20) | copy-start | bytes 4718596
Sparse Core Ops, SparseCore 0:
  10.8 77.8 all-gather.8
  90.5 80.5 all-gather.4
  172.9 56.0 all-gather.6
where the time goes:
time: 490 us; the launch traced here: 489 us
  waiting for transfers between devices  257 us (52%)
  blocking collectives  99.6 us (20%)
  local copies, waits for them, and re-layouts  42 us (9%)
  other arithmetic  36.3 us (7%)
  matrix products  28.7 us (6%)
  between operations  14.2 us (3%)
  starting transfers between devices  11.9 us (2%)
    all_to_all x1, blocking collectives, shards(): arrived = lax.all_to_all(outgoing, 'chip', 0, 0, tiled=True)  99.6 us
    all_to_all x1, waiting for transfers between devices, shards(): returned = lax.all_to_all(summed, 'chip', 0, 0, tiled=True)  90.3 us
    all_gather x1, waiting for transfers between devices, shards(): lax.all_gather(qkv_weight, 'dp', axis=1, tiled=True)  71.2 us
    all_gather x1, waiting for transfers between devices, shards(): piece = lax.all_gather(prefix_cache[0], TENSOR, axis=0, tiled=True)  57.8 us
    ppermute x2, waiting for transfers between devices, from_behind(): lax.ppermute(value, axis, [(source, source + steps) for source in range(f...  11.2 us
    all_gather x1, waiting for transfers between devices, shards(): lax.all_gather(out_weight, 'dp', axis=0, tiled=True)  10.7 us
    another operation x6, other arithmetic  10.2 us
    gather x1, local copies, waits for them, and re-layouts, shards(): returned.reshape(chips * CAP, model)[target].reshape(rows, TOPK, model)  10 us
  transfers between devices with their start and end apart: 8, of which 8 were waited for; matrix products, arithmetic and copies ran while one was open for 13% of the time, Pallas kernels for 0%

commit v1 on v0

--- a/solution.py
+++ b/solution.py
@@ -13,6 +13,24 @@
 TENSOR = ("chip", "core")
 EPS = 1e-06
 THETA = 10000.0
+
+
+def ring_gather(shard, axis, dim):
+    ways, here, hop = (lax.axis_size(axis), lax.axis_index(axis), shard.shape[dim])
+    dims = [n * ways if d == dim else n for d, n in enumerate(shard.shape)]
+    full = lax.dynamic_update_slice_in_dim(
+        jnp.zeros(dims, shard.dtype), shard, here * hop, axis=dim
+    )
+    going_up = going_down = shard
+    for far in range(1, ways // 2 + 1):
+        going_up = lax.ppermute(going_up, axis, [(d, (d + 1) % ways) for d in range(ways)])
+        full = lax.dynamic_update_slice_in_dim(full, going_up, (here - far) % ways * hop, axis=dim)
+        if 2 * far < ways:
+            going_down = lax.ppermute(going_down, axis, [(d, (d - 1) % ways) for d in range(ways)])
+            full = lax.dynamic_update_slice_in_dim(
+                full, going_down, (here + far) % ways * hop, axis=dim
+            )
+    return full
 
 
 def from_behind(value, axis, steps):
@@ -87,7 +105,7 @@
     normed = rms_norm(inputs, attn_gain)
     full_qkv, full_out = (
         lax.all_gather(qkv_weight, "dp", axis=1, tiled=True),
-        lax.all_gather(out_weight, "dp", axis=0, tiled=True),
+        ring_gather(out_weight, "dp", 0),
     )
     qkv = jnp.dot(normed, full_qkv, preferred_element_type=jnp.float32).astype(jnp.bfloat16)
     lane = lax.axis_index(TENSOR)

time: 490 us -> 476 us (0.971)
  waiting for transfers between devices: 257 us -> 231 us
  local copies, waits for them, and re-layouts: 42 us -> 51.3 us
    all_gather x1, waiting for transfers between devices: 57.8 us -> 40.8 us  [shards(): piece = lax.all_gather(prefix_cache[0], TENSOR, axis=0, tiled=True)]
    all_gather x1 -> x0, waiting for transfers between devices: 10.7 us -> none  [shards(): lax.all_gather(out_weight, 'dp', axis=0, tiled=True)]
    dynamic_update_slice x0 -> x4, local copies, waits for them, and re-layouts: none -> 9.54 us  [the longest x2 4.79 us: ring_gather(): lax.dynamic_update_slice_in_dim(full, going_up, (here - far) % ways * hop...]
    ppermute x0 -> x3, waiting for transfers between devices: none -> 5.59 us  [the longest x2 5.59 us: ring_gather(): lax.ppermute(going_up, axis, [(d, (d + 1) % ways) for d in range(ways)])]
  transfers between devices with their start and end apart: 8 -> 10, of which waited for: 8 -> 8; matrix products, arithmetic and copies ran while one was open for 13% -> 10% of each run, Pallas kernels for 0% -> 0%
where the time goes in v1:
time: 476 us; the launch traced here: 472 us
  waiting for transfers between devices  231 us (49%)
  blocking collectives  98.5 us (21%)
  local copies, waits for them, and re-layouts  51.3 us (11%)
  other arithmetic  33.2 us (7%)
  matrix products  27.7 us (6%)
  starting transfers between devices  15.4 us (3%)
  between operations  14.5 us (3%)
    all_to_all x1, blocking collectives, shards(): arrived = lax.all_to_all(outgoing, 'chip', 0, 0, tiled=True)  98.5 us
    all_to_all x1, waiting for transfers between devices, shards(): returned = lax.all_to_all(summed, 'chip', 0, 0, tiled=True)  88.7 us
    all_gather x1, waiting for transfers between devices, shards(): lax.all_gather(qkv_weight, 'dp', axis=1, tiled=True)  68.9 us
    all_gather x1, waiting for transfers between devices, shards(): piece = lax.all_gather(prefix_cache[0], TENSOR, axis=0, tiled=True)  40.8 us
    ppermute x2, waiting for transfers between devices, from_behind(): lax.ppermute(value, axis, [(source, source + steps) for source in range(f...  12.3 us
    another operation x6, other arithmetic  10.2 us
    gather x1, local copies, waits for them, and re-layouts, shards(): returned.reshape(chips * CAP, model)[target].reshape(rows, TOPK, model)  10 us
  transfers between devices with their start and end apart: 10, of which 8 were waited for; matrix products, arithmetic and copies ran while one was open for 10% of the time, Pallas kernels for 0%

profile of v1, /device:TPU:34, one launch (start us, length us, event | category | flops | bytes accessed | tf_op | source)
XLA Modules:
  0.0 471.8 jit_solution(16015862847628143762)
XLA Ops:
  8.7 1.7 collective-permute-start.2
  10.3 1.7 collective-permute-start.3
  13.0 1.0 reduce-window.15
  15.0 9.0 %reduce-window.19 = s32[32,8,128]{2,1,0:T(8,128)S(1)} reduce-window(s32[32,8,128]{2,1,0:T(8,128)S(1)} %fusion.64, s32[]{:T(128)} %constant.81.clone.1), window={size=1x1x128 pad=0_0x0_0x127_0}, to_apply=%region_11.12 | reduce-window | flops 4161536 | bytes 262148 | tf_op jit(solution)/shard_map/reduce-window.2
  24.6 4.3 scatter_custom_fusion
  31.6 0.9 compare_and_fusion
  32.5 5.6 %collective-permute-done.2 = bf16[384,1536]{1,0:T(8,128)(2,1)} collective-permute-done((bf16[384,1536]{1,0:T(8,128)(2,1)}, bf16[384,1536]{1,0:T(8,128)(2,1)}, u32[]{:S(2)}, u32[]{:S(2)}) %collective-permute-start.2) | collective-permute-done | bytes 1179680 | tf_op jit(solution)/shard_map/ppermute | solution.py:26
  38.4 2.4 broadcast_in_dim.99
  40.8 2.4 constant_dynamic-update-slice_fusion.3
  43.1 2.4 constant_dynamic-update-slice_fusion.2
  45.5 2.4 constant_dynamic-update-slice_fusion.1
  47.9 40.8 %all-gather.6.cloned.1.call-done = bf16[1,512,2,512]{3,2,0,1:T(2,128)(2,1)} async-done(((bf16[1,8,2,512]{3,2,0,1:T(2,128)(2,1)}), bf16[1,512,2,512]{3,2,0,1:T(2,128)(2,1)}) %all-gather.6.cloned.1.call-update) | async-done | bytes 1048592 | tf_op jit(solution)/shard_map/all_gather | solution.py:131
  88.7 4.1 fusion.74
  92.8 3.5 copy.57
  96.3 3.5 copy.58
  99.8 2.4 constant_dynamic-update-slice_fusion
  102.2 68.9 %all-gather.4.cloned.1.call-done = bf16[1536,2560]{1,0:T(8,128)(2,1)} async-done(((bf16[1536,640]{1,0:T(8,128)(2,1)}), bf16[1536,2560]{1,0:T(8,128)(2,1)}) %all-gather.4.cloned.1.call-update) | async-done | bytes 7864336 | tf_op jit(solution)/shard_map/all_gather | solution.py:107
  171.1 4.5 convolution_convert_fusion.1
  177.5 1.9 collective-permute-start
  179.8 5.7 %collective-permute-done = bf16[1,128,2,512]{3,1,2,0:T(8,128)(2,1)} collective-permute-done((bf16[1,128,2,512]{3,1,2,0:T(8,128)(2,1)}, bf16[1,128,2,512]{3,1,2,0:T(8,128)(2,1)}, u32[]{:S(2)}, u32[]{:S(2)}) %collective-permute-start) | collective-permute-done | bytes 262176 | tf_op jit(solution)/shard_map/ppermute | solution.py:39
  185.5 1.1 pad_maximum_fusion.2
  186.6 3.6 collective-permute-start.1
  190.2 0.9 fusion.51
  191.2 3.7 bitcast_reduce_fusion
  194.9 6.6 %collective-permute-done.1 = bf16[2,128,2,512]{3,1,2,0:T(8,128)(2,1)S(1)} collective-permute-done((bf16[2,128,2,512]{3,1,2,0:T(8,128)(2,1)S(1)}, bf16[2,128,2,512]{3,1,2,0:T(8,128)(2,1)S(1)}, u32[]{:S(2)}, u32[]{:S(2)}) %collective-permute-start.1) | collective-permute-done | bytes 524320 | tf_op jit(solution)/shard_map/ppermute | solution.py:39
  201.5 1.1 pad_maximum_fusion.1
  202.7 0.9 fusion.75
  203.6 1.0 copy.64
  204.6 1.3 copy.63
  205.8 1.1 fusion.2
  207.0 1.5 fusion.5
  208.5 1.7 fusion.22
  210.3 1.6 fusion.3
  211.9 1.7 fusion.40
  213.6 3.2 fusion.43
  217.1 5.4 %gather_fusion = bf16[1280,1536]{1,0:T(8,128)(2,1)} fusion(bf16[129,1536]{1,0:T(8,128)(2,1)S(1)} %concatenate.40, s32[2048]{0:T(1024)S(1)} %pad_clamp_fusion), kind=kCustom, calls=%fused_computation | custom fusion | bytes 7869440 | tf_op jit(solution)/shard_map/gather | solution.py:175
  222.6 98.5 %all_to_all.10 = bf16[32,40,1536]{2,1,0:T(8,128)(2,1)S(1)} all-to-all(bf16[32,40,1536]{2,1,0:T(8,128)(2,1)} %bitcast.159), channel_id=1, replica_groups=mesh['dp'=4,'chip'=32,'core'=2] {'chip'}, dimensions={0} | all-to-all | bytes 7864320 | tf_op jit(solution)/shard_map/all_to_all | solution.py:176
  321.0 2.0 copy-done.2
  323.0 6.9 %collective-permute-done.5 = bf16[32,40,1536]{2,1,0:T(8,128)(2,1)} collective-permute-done((bf16[32,40,1536]{2,1,0:T(8,128)(2,1)S(1)}, bf16[32,40,1536]{2,1,0:T(8,128)(2,1)}, u32[]{:S(2)}, u32[]{:S(2)}) %collective-permute-start.5) | collective-permute-done | bytes 3932192 | tf_op jit(solution)/shard_map/ppermute | solution.py:177
  329.9 7.1 %pad_maximum_fusion = bf16[64,40,1536]{2,1,0:T(8,128)(2,1)} fusion(bf16[32,40,1536]{2,1,0:T(8,128)(2,1)} %collective-permute-done.5, bf16[32,40,1536]{2,1,0:T(8,128)(2,1)} %copy-done.2), kind=kLoop, calls=%fused_computation.4 | loop fusion | flops 3932160 | bytes 15728640 | tf_op jit(solution)/shard_map/concatenate | solution.py:178
  337.0 6.6 %fusion.18 = f32[2560,512]{1,0:T(8,128)S(1)} fusion(bf16[2560,1536]{1,0:T(8,128)(2,1)} %bitcast.161, bf16[1,1536,512]{2,1,0:T(8,128)(2,1)S(1)} %copy-done), kind=kOutput, calls=%fused_computation.29 | convolution fusion | flops 4026531840 | bytes 14680064 | tf_op jit(solution)/shard_map/dot_general | solution.py:179
  343.6 2.3 convolution_convert_fusion
  346.7 6.6 %collective-permute-done.6 = bf16[32,40,1536]{2,1,0:T(8,128)(2,1)S(1)} collective-permute-done((bf16[32,40,1536]{2,1,0:T(8,128)(2,1)S(1)}, bf16[32,40,1536]{2,1,0:T(8,128)(2,1)S(1)}, u32[]{:S(2)}, u32[]{:S(2)}) %collective-permute-start.6) | collective-permute-done | bytes 3932192 | tf_op jit(solution)/shard_map/ppermute | solution.py:185
  353.3 3.0 fusion
  356.3 6.0 %all-to-all-start.1 = ((bf16[32,40,1536]{2,1,0:T(8,128)(2,1)}), bf16[32,40,1536]{2,1,0:T(8,128)(2,1)}, u32[]{:S(2)}, u32[]{:S(2)}) async-start(bf16[32,40,1536]{2,1,0:T(8,128)(2,1)} %fusion), calls=%async_computation.1 | async-start | bytes 7864320 | tf_op jit(solution)/shard_map/all_to_all | solution.py:187
  362.5 88.7 %all-to-all-done.1 = bf16[32,40,1536]{2,1,0:T(8,128)(2,1)} async-done(((bf16[32,40,1536]{2,1,0:T(8,128)(2,1)}), bf16[32,40,1536]{2,1,0:T(8,128)(2,1)}, u32[]{:S(2)}, u32[]{:S(2)}) %all-to-all-start.1) | async-done | bytes 3932192 | tf_op jit(solution)/shard_map/all_to_all | solution.py:187
  451.2 10.0 %gather_fusion.1 = bf16[1024,1536]{1,0:T(8,128)(2,1)} fusion(bf16[1280,1536]{1,0:T(8,128)(2,1)} %bitcast.47, s32[1024]{0:T(1024)S(1)} %broadcast_clamp_fusion), kind=kCustom, calls=%fused_computation.1 | custom fusion | bytes 6295552 | tf_op jit(solution)/shard_map/gather | solution.py:188
  461.2 2.8 fusion.9
  (98 shorter events, 11.3 us)
Async XLA Ops:
  7.2 329.8 %copy-start = (bf16[1,1536,512]{2,1,0:T(8,128)(2,1)S(1)}, bf16[1,1536,512]{2,1,0:T(8,128)(2,1)}, u32[]{:S(2)}) copy-start(bf16[1,1536,512]{2,1,0:T(8,128)(2,1)} %param.20) | copy-start | bytes 4718596
  7.2 24.1 %copy-start.3 = (bf16[1,128,1536]{2,1,0:T(8,128)(2,1)S(1)}, bf16[1,128,1536]{2,1,0:T(8,128)(2,1)}, u32[]{:S(2)}) copy-start(bf16[1,128,1536]{2,1,0:T(8,128)(2,1)} %param.11) | copy-start | bytes 1179652
  7.2 81.5 %all-gather.6.cloned.1.call-start = ((), (), s32[]{:S(2)}) async-start(), calls=%async_computation.3 | async-start | bytes 1064960 | tf_op jit(solution)/shard_map/all_gather | solution.py:131
  7.9 163.2 %all-gather.4.cloned.1.call-start = ((), (), s32[]{:S(2)}) async-start(), calls=%async_computation.2 | async-start | bytes 9830400 | tf_op jit(solution)/shard_map/all_gather | solution.py:107
  8.7 29.4 %collective-permute-start.2 = (bf16[384,1536]{1,0:T(8,128)(2,1)}, bf16[384,1536]{1,0:T(8,128)(2,1)}, u32[]{:S(2)}, u32[]{:S(2)}) collective-permute-start(bf16[384,1536]{1,0:T(8,128)(2,1)} %param.14), channel_id=1, source_target_pairs={{0,64},{64,128},{128,192},{192,0},{1,65},{65,129},{129,193},{193,1... | collective-permute-start | bytes 3538952 | tf_op jit(solution)/shard_map/ppermute | solution.py:26
  10.3 35.2 %collective-permute-start.3 = (bf16[384,1536]{1,0:T(8,128)(2,1)}, bf16[384,1536]{1,0:T(8,128)(2,1)}, u32[]{:S(2)}, u32[]{:S(2)}) collective-permute-start(bf16[384,1536]{1,0:T(8,128)(2,1)} %param.14), channel_id=1, source_target_pairs={{0,192},{64,0},{128,64},{192,128},{1,193},{65,1},{129,65},{193,129... | collective-permute-start | bytes 3538952 | tf_op jit(solution)/shard_map/ppermute | solution.py:29
  30.8 14.7 %copy-start.9 = (f32[128,64]{0,1:T(8,128)}, f32[128,64]{0,1:T(8,128)S(1)}, u32[]{:S(2)}) copy-start(f32[128,64]{0,1:T(8,128)S(1)} %get-tuple-element.29) | copy-start | bytes 98308
  38.1 61.7 %collective-permute-start.4 = (bf16[384,1536]{1,0:T(8,128)(2,1)}, bf16[384,1536]{1,0:T(8,128)(2,1)}, u32[]{:S(2)}, u32[]{:S(2)}) collective-permute-start(bf16[384,1536]{1,0:T(8,128)(2,1)} %collective-permute-done.2), channel_id=1, source_target_pairs={{0,64},{64,128},{128,192},{192,0},{1,65},{65,129},{129,193},{193,1... | collective-permute-start | bytes 3538952 | tf_op jit(solution)/shard_map/ppermute | solution.py:26
  88.7 82.4 %copy-start.10 = (f32[1536]{0:T(1024)S(1)}, f32[1536]{0:T(1024)}, u32[]{:S(2)}) copy-start(f32[1536]{0:T(1024)} %param.12) | copy-start | bytes 18436
  177.5 8.0 %collective-permute-start = (bf16[1,128,2,512]{3,1,2,0:T(8,128)(2,1)}, bf16[1,128,2,512]{3,1,2,0:T(8,128)(2,1)}, u32[]{:S(2)}, u32[]{:S(2)}) collective-permute-start(bf16[1,128,2,512]{3,1,2,0:T(8,128)(2,1)} %maximum_bitcast_fusion), channel_id=1, source_target_pairs={{0,1},{1,2},{2,3},{3,4},{4,5},{5,6},{6,7},{7,8},{8,9},{9,10},{10,1... | collective-permute-start | bytes 786440 | tf_op jit(solution)/shard_map/ppermute | solution.py:39
  179.8 11.4 %copy-start.5 = (bf16[512,1,512]{0,2,1:T(8,128)(2,1)S(1)}, bf16[512,1,512]{0,2,1:T(8,128)(2,1)}, u32[]{:S(2)}) copy-start(bf16[512,1,512]{0,2,1:T(8,128)(2,1)} %copy.57) | copy-start | bytes 1572868
  186.6 14.9 %collective-permute-start.1 = (bf16[2,128,2,512]{3,1,2,0:T(8,128)(2,1)S(1)}, bf16[2,128,2,512]{3,1,2,0:T(8,128)(2,1)S(1)}, u32[]{:S(2)}, u32[]{:S(2)}) collective-permute-start(bf16[2,128,2,512]{3,1,2,0:T(8,128)(2,1)S(1)} %pad_maximum_fusion.2), channel_id=1, source_target_pairs={{0,2},{1,3},{2,4},{3,5},{4,6},{5,7},{6,8},{7,9},{8,10},{9,11},{10,... | collective-permute-start | bytes 1572872 | tf_op jit(solution)/shard_map/ppermute | solution.py:39
  194.9 11.0 %copy-start.6 = (pred[128,512]{0,1:T(8,128)(4,1)S(1)}, pred[128,512]{0,1:T(8,128)(4,1)}, u32[]{:S(2)}) copy-start(pred[128,512]{0,1:T(8,128)(4,1)} %compare_and_fusion) | copy-start | bytes 196612
  206.9 1.6 copy-start.8
  207.0 3.3 slice-start
  208.5 1.8 slice-start.1
  210.2 1.7 copy-start.7
  213.6 3.3 copy-start.11
  216.9 247.2 %copy-start.4 = (bf16[128,1536]{1,0:T(8,128)(2,1)}, bf16[128,1536]{1,0:T(8,128)(2,1)S(1)}, u32[]{:S(2)}) copy-start(bf16[128,1536]{1,0:T(8,128)(2,1)S(1)} %get-tuple-element.28) | copy-start | bytes 1179652
  321.0 2.0 copy-start.2
  323.0 6.9 %collective-permute-start.5 = (bf16[32,40,1536]{2,1,0:T(8,128)(2,1)S(1)}, bf16[32,40,1536]{2,1,0:T(8,128)(2,1)}, u32[]{:S(2)}, u32[]{:S(2)}) collective-permute-start(bf16[32,40,1536]{2,1,0:T(8,128)(2,1)S(1)} %all_to_all.10), channel_id=1, source_target_pairs={{0,1},{1,0},{2,3},{3,2},{4,5},{5,4},{6,7},{7,6},{8,9},{9,8},{10,11... | collective-permute-start | bytes 11796488 | tf_op jit(solution)/shard_map/ppermute | solution.py:177
  337.0 6.6 %copy-start.13 = (bf16[1,256,1536]{2,1,0:T(8,128)(2,1)S(1)}, bf16[1,256,1536]{2,1,0:T(8,128)(2,1)}, u32[]{:S(2)}) copy-start(bf16[1,256,1536]{2,1,0:T(8,128)(2,1)} %param.21) | copy-start | bytes 2359300
  346.5 6.9 %collective-permute-start.6 = (bf16[32,40,1536]{2,1,0:T(8,128)(2,1)S(1)}, bf16[32,40,1536]{2,1,0:T(8,128)(2,1)S(1)}, u32[]{:S(2)}, u32[]{:S(2)}) collective-permute-start(bf16[32,40,1536]{2,1,0:T(8,128)(2,1)S(1)} %bitcast.166), channel_id=1, source_target_pairs={{0,1},{1,0},{2,3},{3,2},{4,5},{5,4},{6,7},{7,6},{8,9},{9,8},{10,11... | collective-permute-start | bytes 11796488 | tf_op jit(solution)/shard_map/ppermute | solution.py:185
  356.3 6.0 %copy-start.12 = (f32[1,128,8]{1,2,0:T(8,128)S(1)}, f32[1,128,8]{1,2,0:T(8,128)}, u32[]{:S(2)}) copy-start(f32[1,128,8]{1,2,0:T(8,128)} %param.19) | copy-start | bytes 12292
  356.3 94.9 %all-to-all-start.1 = ((bf16[32,40,1536]{2,1,0:T(8,128)(2,1)}), bf16[32,40,1536]{2,1,0:T(8,128)(2,1)}, u32[]{:S(2)}, u32[]{:S(2)}) async-start(bf16[32,40,1536]{2,1,0:T(8,128)(2,1)} %fusion), calls=%async_computation.1 | async-start | bytes 7864320 | tf_op jit(solution)/shard_map/all_to_all | solution.py:187
  451.2 13.7 %copy-start.1 = (bf16[1,1536,512]{2,1,0:T(8,128)(2,1)S(1)}, bf16[1,1536,512]{2,1,0:T(8,128)(2,1)}, u32[]{:S(2)}) copy-start(bf16[1,1536,512]{2,1,0:T(8,128)(2,1)} %param.20) | copy-start | bytes 4718596
Sparse Core Ops, SparseCore 0:
  10.8 77.8 all-gather.5
  90.5 80.5 all-gather.3
